TPU v7x, 256 devices: a whole 4x4x8 slice. The times are simulated.
256 devices in a mesh: tm: 16 (over z, core), box: 16 (over y, x).
Axes of the slice: x: 4, y: 4, z: 8, core: 2. Of those that a mesh axis runs over, the one named last changes fastest.
Arguments:
- traces: bfloat16 [6, 128, 524288], P(None, 'tm', 'box'), may hold values from -6 to 6
- projection: bfloat16 [16, 256, 128, 128], P('box', 'tm'), may hold values from -0.5 to 0.5
- owner_route: int32 [16, 256, 1], P('box', 'tm'), may hold values from 0 to 15; in each aligned block of 16 rows (0 to 15, 16 to 31, ..., all dimensions but the last counted through in order) at most 2 rows name the same one
- face_slot: int32 [16, 256, 1], P('box', 'tm'), may hold values from 0 to 3
- face_weight: float32 [1024, 128], P(('tm', 'box')), may hold values from 0.2 to 2
Outputs:
- face_load: bfloat16 [1024, 6, 128, 128], P(('tm', 'box'))
Inputs may be any that keep to these rules, and one draw needn't show every extreme that they name: `owner_route`: in the aligned blocks of 16 rows (the rows of one device), no owner is named by more than 2 rows, a bound that some block reaches.
All inputs are finite; a program needn't handle non-finite values.
Results may differ from a plain program's by a relative error of at most 0.005.
Values may be sent and summed in bfloat16 or wider, within the bound.
A program may use at most 192 MiB of HBM per device.

v0:
```python
import jax
import jax.numpy as jnp
from jax import lax
from jax.sharding import PartitionSpec as P


def in_blocks(shard, dim, peers):
    dims = shard.shape
    parts = shard.reshape(*dims[:dim], peers, dims[dim] // peers, *dims[dim + 1 :])
    return jnp.moveaxis(parts, dim, 0)


def cut_rows(length, count):
    step = length // count
    if step >= 8:
        step -= step % 8
    return [step * k for k in range(1, count)]


def in_order(parts, dim):
    parts = jnp.moveaxis(parts, 0, dim)
    dims = parts.shape
    return parts.reshape(*dims[:dim], dims[dim] * dims[dim + 1], *dims[dim + 2 :])


def exchange_in_pieces(shard, axis, pieces, split_dim, concat_dim):
    parts = in_blocks(shard, split_dim, lax.axis_size(axis))
    cut = max(range(1, max(2, parts.ndim - 1)), key=lambda d: parts.shape[d])
    finished = []
    for piece in jnp.split(parts, cut_rows(parts.shape[cut], pieces), axis=cut):
        if piece.size:
            finished.append(lax.all_to_all(piece, axis, split_axis=0, concat_axis=0, tiled=True))
    return in_order(jnp.concatenate(finished, axis=cut), concat_dim)


def ranks_within(owners):
    blocks = owners.shape[-1]
    same = owners[..., :, None] == owners[..., None, :]
    before = jnp.arange(blocks)[None, :] < jnp.arange(blocks)[:, None]
    return jnp.sum((same & before).astype(jnp.int32), axis=-1)


def per_device(traces, projection, owner_route, face_slot, face_weight):
    nodes = projection.shape[-1]
    blocks = projection.shape[1]
    slots_dev = face_weight.shape[0]
    boxes = lax.axis_size("box")
    bucket = blocks // boxes + 1
    matrices = projection[0]
    pointwise = exchange_in_pieces(traces, "tm", 2, 2, 1)
    count = pointwise.shape[0]
    shaped = pointwise.reshape(count, pointwise.shape[1], blocks, nodes)
    result = jnp.einsum("csjn,jnm->jcsm", shaped, matrices, preferred_element_type=jnp.float32)
    faces = result.astype(jnp.bfloat16)
    own_owner = owner_route[0, :, 0]
    own_slot = face_slot[0, :, 0]
    own_rank = ranks_within(own_owner)
    target_owner = jnp.arange(boxes)[:, None, None]
    target_rank = jnp.arange(bucket)[None, :, None]
    chosen = (own_owner[None, None, :] == target_owner) & (own_rank[None, None, :] == target_rank)
    chosen = chosen.reshape(boxes * bucket, blocks)
    picker = chosen.astype(jnp.bfloat16)
    outgoing = jnp.einsum(
        "kj,jcsn->kcsn", picker, faces, preferred_element_type=jnp.float32
    ).astype(jnp.bfloat16)
    outgoing = outgoing.reshape((boxes, bucket) + faces.shape[1:])
    samples = faces.shape[2]
    filled = jnp.sum(chosen.astype(jnp.float32), axis=1)
    slot_sum = jnp.sum(chosen.astype(jnp.float32) * own_slot[None, :].astype(jnp.float32), axis=1)
    tag_value = slot_sum + (filled - 1.0)
    tag_grid = jnp.broadcast_to(
        tag_value.reshape(boxes, bucket, 1, 1, 1), (boxes, bucket, 1, samples, 1)
    ).astype(jnp.bfloat16)
    arrived = lax.all_to_all(outgoing, "box", split_axis=0, concat_axis=0, tiled=True)
    tagged = lax.all_to_all(tag_grid, "box", split_axis=0, concat_axis=0, tiled=True)
    width = arrived.shape[3]
    flat = arrived.reshape((boxes * bucket,) + arrived.shape[2:])
    tag_flat = tagged.reshape(boxes * bucket, width).astype(jnp.float32)
    placing = (
        tag_flat[None, :, :] == jnp.arange(slots_dev, dtype=jnp.float32)[:, None, None]
    ).astype(jnp.bfloat16)
    gathered = jnp.einsum("fks,kcsn->fcsn", placing, flat, preferred_element_type=jnp.float32)
    return (gathered * face_weight[:, None, None, :]).astype(jnp.bfloat16)


def solution(mesh):
    return jax.shard_map(
        per_device,
        mesh=mesh,
        in_specs=(
            P(None, "tm", "box"),
            P("box", "tm", None, None),
            P("box", "tm", None),
            P("box", "tm", None),
            P(("tm", "box"), None),
        ),
        out_specs=P(("tm", "box"), None, None, None),
        check_vma=False,
    )
```

profile of v0, /device:TPU:1, one launch (start us, length us, event | category | flops | bytes accessed | tf_op | source)
XLA Modules:
  0.0 231.4 jit_solution(14159657702393699322)
XLA Ops:
  0.0 0.0 copy-start
  0.0 3.9 %copy.41 = bf16[6,8,16,2048]{3,2,1,0:T(8,128)(2,1)S(1)} copy(bf16[6,8,16,2048]{3,1,2,0:T(8,128)(2,1)} %bitcast.47) | data formatting | bytes 6291456
  3.9 1.5 fusion.13
  5.4 2.4 %copy.19 = bf16[16,6,4,2048]{3,2,1,0:T(4,128)(2,1)} copy(bf16[16,6,4,2048]{3,0,2,1:T(8,128)(2,1)S(1)} %get-tuple-element.9) | data formatting | bytes 3145728 | tf_op jit(solution)/shard_map/split | solution.py:30
  7.8 10.0 %all-to-all-start.1 = ((bf16[16,6,4,2048]{3,2,1,0:T(4,128)(2,1)}), bf16[16,6,4,2048]{3,2,1,0:T(4,128)(2,1)S(1)}, u32[]{:S(2)}, u32[]{:S(2)}) async-start(bf16[16,6,4,2048]{3,2,1,0:T(4,128)(2,1)} %copy.19), calls=%async_computation.1 | async-start | bytes 3145728 | tf_op jit(solution)/shard_map/all_to_all | solution.py:32
  17.8 0.0 copy-start.1
  17.8 0.0 copy-start.3
  17.8 3.8 %copy.18 = bf16[16,6,4,2048]{3,2,1,0:T(4,128)(2,1)} copy(bf16[16,6,4,2048]{3,0,2,1:T(8,128)(2,1)} %get-tuple-element.8) | data formatting | bytes 3145728 | tf_op jit(solution)/shard_map/split | solution.py:30
  21.6 34.7 %all-to-all-done.1 = bf16[16,6,4,2048]{3,2,1,0:T(4,128)(2,1)S(1)} async-done(((bf16[16,6,4,2048]{3,2,1,0:T(4,128)(2,1)}), bf16[16,6,4,2048]{3,2,1,0:T(4,128)(2,1)S(1)}, u32[]{:S(2)}, u32[]{:S(2)}) %all-to-all-start.1) | async-done | bytes 1572896 | tf_op jit(solution)/shard_map/all_to_all | solution.py:32
  56.3 4.3 %all-to-all-start = ((bf16[16,6,4,2048]{3,2,1,0:T(4,128)(2,1)}), bf16[16,6,4,2048]{3,2,1,0:T(4,128)(2,1)}, u32[]{:S(2)}, u32[]{:S(2)}) async-start(bf16[16,6,4,2048]{3,2,1,0:T(4,128)(2,1)} %copy.18), calls=%async_computation | async-start | bytes 3145728 | tf_op jit(solution)/shard_map/all_to_all | solution.py:32
  60.6 0.0 copy-done.1
  60.6 0.2 convert_reduce_fusion.1
  60.8 0.0 copy-done.3
  60.8 0.1 convert_reduce_fusion
  61.0 38.1 %all-to-all-done = bf16[16,6,4,2048]{3,2,1,0:T(4,128)(2,1)} async-done(((bf16[16,6,4,2048]{3,2,1,0:T(4,128)(2,1)}), bf16[16,6,4,2048]{3,2,1,0:T(4,128)(2,1)}, u32[]{:S(2)}, u32[]{:S(2)}) %all-to-all-start) | async-done | bytes 1572896 | tf_op jit(solution)/shard_map/all_to_all | solution.py:32
  99.1 0.7 broadcast_in_dim.2
  99.7 6.8 %all-to-all-start.3 = ((bf16[16,2,1,128,1]{3,1,4,2,0:T(2,128)(2,1)}), bf16[16,2,1,128,1]{3,1,4,2,0:T(2,128)(2,1)S(1)}, u32[]{:S(2)}, u32[]{:S(2)}) async-start(bf16[16,2,1,128,1]{3,1,4,2,0:T(2,128)(2,1)} %broadcast_in_dim.2), calls=%async_computation.3 | async-start | bytes 16384 | tf_op jit(solution)/shard_map/all_to_all | solution.py:75
  106.5 3.0 %maximum_bitcast_fusion = bf16[6,16,8,2048]{3,2,0,1:T(8,128)(2,1)S(1)} fusion(bf16[16,6,4,2048]{3,2,1,0:T(4,128)(2,1)S(1)} %all-to-all-done.1, bf16[16,6,4,2048]{3,2,1,0:T(4,128)(2,1)} %all-to-all-done), kind=kLoop, calls=%fused_computation.2 | loop fusion | flops 6291456 | bytes 6291456 | tf_op jit(solution)/shard_map/transpose | solution.py:21
  109.6 0.4 copy.20
  110.0 1.0 copy.33
  111.0 0.0 copy-done
  111.0 1.0 fusion.3
  112.0 2.5 %convolution_convert_fusion = bf16[32,6,128,128]{3,0,2,1:T(8,128)(2,1)S(1)} fusion(bf16[16,6,128,128]{3,2,1,0:T(8,128)(2,1)S(1)} %fusion.3, pred[32,16]{1,0:T(32,128)(4,1)S(1)} %and.26), kind=kOutput, calls=%fused_computation | convolution fusion | flops 103809024 | bytes 9437696 | tf_op jit(solution)/shard_map/kj,jcsn->kcsn/dot_general | solution.py:63
  114.5 5.4 %copy.24 = bf16[16,2,6,128,128]{4,1,3,2,0:T(2,128)(2,1)} copy(bf16[16,2,6,128,128]{4,1,0,3,2:T(2,128)(2,1)S(1)} %bitcast.42) | data formatting | bytes 12582912 | tf_op jit(solution)/shard_map/reshape | solution.py:66
  119.9 0.0 all-to-all-done.3
  119.9 6.7 %all-to-all-start.2 = ((bf16[16,2,6,128,128]{4,1,3,2,0:T(2,128)(2,1)}), bf16[16,2,6,128,128]{4,1,3,2,0:T(2,128)(2,1)}, u32[]{:S(2)}, u32[]{:S(2)}) async-start(bf16[16,2,6,128,128]{4,1,3,2,0:T(2,128)(2,1)} %copy.24), calls=%async_computation.2 | async-start | bytes 12582912 | tf_op jit(solution)/shard_map/all_to_all | solution.py:74
  126.6 0.1 copy.26
  126.7 0.0 copy-start.2
  126.7 94.8 %all-to-all-done.2 = bf16[16,2,6,128,128]{4,1,3,2,0:T(2,128)(2,1)} async-done(((bf16[16,2,6,128,128]{4,1,3,2,0:T(2,128)(2,1)}), bf16[16,2,6,128,128]{4,1,3,2,0:T(2,128)(2,1)}, u32[]{:S(2)}, u32[]{:S(2)}) %all-to-all-start.2) | async-done | bytes 6291488 | tf_op jit(solution)/shard_map/all_to_all | solution.py:74
  221.5 7.8 %copy.25 = bf16[16,2,6,128,128]{4,1,0,2,3:T(2,128)(2,1)S(1)} copy(bf16[16,2,6,128,128]{4,1,3,2,0:T(2,128)(2,1)} %all-to-all-done.2) | data formatting | bytes 12582912 | tf_op jit(solution)/shard_map/all_to_all | solution.py:74
  229.3 0.0 copy-done.2
  229.4 0.9 fusion.6
  230.3 1.1 copy.27
  (5 shorter events, 0.0 us)
Async XLA Ops:
  0.0 111.0 %copy-start = (bf16[1,16,128,128]{3,2,1,0:T(8,128)(2,1)S(1)}, bf16[1,16,128,128]{3,2,1,0:T(8,128)(2,1)}, u32[]{:S(2)}) copy-start(bf16[1,16,128,128]{3,2,1,0:T(8,128)(2,1)} %param.6) | copy-start | bytes 1572868
  7.8 48.5 %all-to-all-start.1 = ((bf16[16,6,4,2048]{3,2,1,0:T(4,128)(2,1)}), bf16[16,6,4,2048]{3,2,1,0:T(4,128)(2,1)S(1)}, u32[]{:S(2)}, u32[]{:S(2)}) async-start(bf16[16,6,4,2048]{3,2,1,0:T(4,128)(2,1)} %copy.19), calls=%async_computation.1 | async-start | bytes 3145728 | tf_op jit(solution)/shard_map/all_to_all | solution.py:32
  17.8 42.8 %copy-start.1 = (s32[1,16,1]{1,2,0:T(1,128)S(1)}, s32[1,16,1]{1,2,0:T(1,128)}, u32[]{:S(2)}) copy-start(s32[1,16,1]{1,2,0:T(1,128)} %param.7) | copy-start | bytes 196
  17.8 43.0 %copy-start.3 = (s32[1,16,1]{1,2,0:T(1,128)S(1)}, s32[1,16,1]{1,2,0:T(1,128)}, u32[]{:S(2)}) copy-start(s32[1,16,1]{1,2,0:T(1,128)} %param.8) | copy-start | bytes 196
  56.3 42.8 %all-to-all-start = ((bf16[16,6,4,2048]{3,2,1,0:T(4,128)(2,1)}), bf16[16,6,4,2048]{3,2,1,0:T(4,128)(2,1)}, u32[]{:S(2)}, u32[]{:S(2)}) async-start(bf16[16,6,4,2048]{3,2,1,0:T(4,128)(2,1)} %copy.18), calls=%async_computation | async-start | bytes 3145728 | tf_op jit(solution)/shard_map/all_to_all | solution.py:32
  99.7 20.2 %all-to-all-start.3 = ((bf16[16,2,1,128,1]{3,1,4,2,0:T(2,128)(2,1)}), bf16[16,2,1,128,1]{3,1,4,2,0:T(2,128)(2,1)S(1)}, u32[]{:S(2)}, u32[]{:S(2)}) async-start(bf16[16,2,1,128,1]{3,1,4,2,0:T(2,128)(2,1)} %broadcast_in_dim.2), calls=%async_computation.3 | async-start | bytes 16384 | tf_op jit(solution)/shard_map/all_to_all | solution.py:75
  119.9 101.6 %all-to-all-start.2 = ((bf16[16,2,6,128,128]{4,1,3,2,0:T(2,128)(2,1)}), bf16[16,2,6,128,128]{4,1,3,2,0:T(2,128)(2,1)}, u32[]{:S(2)}, u32[]{:S(2)}) async-start(bf16[16,2,6,128,128]{4,1,3,2,0:T(2,128)(2,1)} %copy.24), calls=%async_computation.2 | async-start | bytes 12582912 | tf_op jit(solution)/shard_map/all_to_all | solution.py:74
  126.7 102.6 %copy-start.2 = (f32[4,128]{1,0:T(4,128)S(1)}, f32[4,128]{1,0:T(4,128)}, u32[]{:S(2)}) copy-start(f32[4,128]{1,0:T(4,128)} %param.9) | copy-start | bytes 6148
where the time goes:
time: 232 us; the launch traced here: 231 us
  waiting for transfers between devices  168 us (72%)
  local copies, waits for them, and re-layouts  28.1 us (12%)
  starting transfers between devices  27.7 us (12%)
  matrix products  4.43 us (2%)
  other arithmetic  3.36 us (1%)
    all_to_all x1, waiting for transfers between devices, per_device(): lax.all_to_all(outgoing, 'box', split_axis=0, concat_axis=0, tiled=True)  94.8 us
    all_to_all x2, waiting for transfers between devices, exchange_in_pieces(): lax.all_to_all(piece, axis, split_axis=0, concat_axis=0, tiled=True)  72.8 us
    all_to_all x2, starting transfers between devices, exchange_in_pieces(): lax.all_to_all(piece, axis, split_axis=0, concat_axis=0, tiled=True)  14.3 us
    all_to_all x1, local copies, waits for them, and re-layouts, per_device(): lax.all_to_all(outgoing, 'box', split_axis=0, concat_axis=0, tiled=True)  7.84 us
    split x3, local copies, waits for them, and re-layouts, exchange_in_pieces(): jnp.split(parts, cut_rows(parts.shape[cut], pieces), axis=cut)  7.71 us
    all_to_all x1, starting transfers between devices, per_device(): lax.all_to_all(tag_grid, 'box', split_axis=0, concat_axis=0, tiled=True)  6.76 us
    all_to_all x1, starting transfers between devices, per_device(): lax.all_to_all(outgoing, 'box', split_axis=0, concat_axis=0, tiled=True)  6.7 us
    reshape x1, local copies, waits for them, and re-layouts, per_device(): outgoing = outgoing.reshape((boxes, bucket) + faces.shape[1:])  5.4 us
  transfers between devices with their start and end apart: 4, of which 3 were waited for; matrix products, arithmetic and copies ran while one was open for 8% of the time, Pallas kernels for 0%

commit v1 on v0

v1 whole, which is shorter than its diff:
```python
import functools

import jax
import jax.numpy as jnp
from jax import lax
from jax.experimental import pallas as pl
from jax.experimental.pallas import tpu as pltpu
from jax.sharding import PartitionSpec as P

MESH = pl.DeviceIdType.MESH
ZS, CS, YS, XS = 8, 2, 4, 4
BLOCKS = 16
OWNERS = YS * XS
CAP = 2
SLOTS = 4
COMP = 6
ROWS = 8
NODES = 128
HALF = COMP * ROWS
COLS = BLOCKS * NODES
STEPS = ZS


def mod(value, size):
    return lax.rem(value + size, jnp.int32(size))


def offset(step):
    return ((step + 1) // 2) * (2 * lax.rem(step, 2) - 1)


def kernel(
    traces, projection, table, weight, out,
    xbuf, pbuf, fbuf, s1a, s1b, r1a, r1b, s2a, s2b, r2a, r2b, s3, r3,
    tabz, taby, tabx,
    xl_sem, xs_sem, xr_sem, pl_sem, ps_sem, pr_sem, tl_sem, tzs_sem, tzr_sem, txs_sem, txr_sem,
    s1s_sem, s1r_sem, s2s_sem, s2r_sem, s3s_sem, s3r_sem,
):
    tm = lax.axis_index("tm")
    box = lax.axis_index("box")
    z, c = tm // CS, lax.rem(tm, CS)
    y, x = box // XS, lax.rem(box, XS)

    def at(zz, cc, yy, xx):
        return {"tm": zz * CS + cc, "box": yy * XS + xx}

    sibling = at(z, 1 - c, y, x)

    def on_z(dz):
        return at(mod(z + dz, ZS), c, y, x)

    def on_y(dy):
        return at(z, c, mod(y + dy, YS), x)

    def on_x(dx):
        return at(z, c, y, mod(x + dx, XS))

    def remote(src, dst, send, recv, device):
        return pltpu.make_async_remote_copy(
            src_ref=src, dst_ref=dst, send_sem=send, recv_sem=recv, device_id=device, device_id_type=MESH
        )

    def cols(step, core):
        row = mod(z + offset(step), ZS) * CS + core
        return pl.ds(pl.multiple_of(row * COLS, COLS), COLS)

    def x_local(step):
        return pltpu.make_async_copy(traces.at[:, :, cols(step, c)], xbuf.at[step, c], xl_sem.at[step])

    def x_remote(step):
        return remote(
            traces.at[:, :, cols(step, 1 - c)], xbuf.at[step, c], xs_sem.at[step], xr_sem.at[step], sibling
        )

    def x_arrival(step):
        return remote(
            traces.at[:, :, cols(step, 1 - c)], xbuf.at[step, 1 - c], xs_sem.at[step], xr_sem.at[step], sibling
        )

    p_local = pltpu.make_async_copy(projection.at[0], pbuf.at[0], pl_sem.at[0])
    p_local.start()

    def start_local(step, carry):
        x_local(step).start()
        return carry

    lax.fori_loop(0, STEPS, start_local, 0)
    t_local = pltpu.make_async_copy(table, tabz.at[0], tl_sem.at[0])
    t_local.start()

    barrier = pltpu.get_barrier_semaphore()
    pl.semaphore_signal(barrier, inc=1, device_id=sibling, device_id_type=MESH)
    for dz in range(1, ZS):
        pl.semaphore_signal(barrier, inc=1, device_id=on_z(dz), device_id_type=MESH)
    for d in range(1, YS):
        pl.semaphore_signal(barrier, inc=1, device_id=on_y(d), device_id_type=MESH)
        pl.semaphore_signal(barrier, inc=1, device_id=on_x(d), device_id_type=MESH)
    pl.semaphore_wait(barrier, 1 + (ZS - 1) + (YS - 1) + (XS - 1))

    p_first = [
        remote(projection.at[0], pbuf.at[1], ps_sem.at[1], pr_sem.at[1], on_z(-1)),
        remote(projection.at[0], pbuf.at[2], ps_sem.at[2], pr_sem.at[2], on_z(1)),
    ]
    x_remote(0).start()
    for copy in p_first:
        copy.start()

    def table_z(step):
        return remote(table, tabz.at[step], tzs_sem.at[step], tzr_sem.at[step], on_z(-offset(step)))

    def start_remote(step, carry):
        table_z(step).start()
        x_remote(step).start()
        return carry

    lax.fori_loop(1, STEPS, start_remote, 0)

    def forward(step, way):
        return remote(pbuf.at[step], pbuf.at[step + 2], ps_sem.at[step + 2], pr_sem.at[step + 2], on_z(way))

    half_p = BLOCKS // 2
    last_low = remote(
        pbuf.at[5, pl.ds(0, half_p)], pbuf.at[7, pl.ds(0, half_p)], ps_sem.at[7], pr_sem.at[7], on_z(-1)
    )
    last_high = remote(
        pbuf.at[6, pl.ds(half_p, half_p)], pbuf.at[7, pl.ds(half_p, half_p)], ps_sem.at[8], pr_sem.at[8], on_z(1)
    )

    def p_arrival(step):
        return remote(pbuf.at[step], pbuf.at[step], ps_sem.at[step], pr_sem.at[step], on_z(1))

    def stage1(step):
        copies = []
        for d in range(1, YS):
            copies.append(remote(
                s1a.at[step, mod(y + d, YS)], r1a.at[step, d - 1],
                s1s_sem.at[step, d - 1], s1r_sem.at[step, d - 1], on_y(d),
            ))
            copies.append(remote(
                s1b.at[step, mod(x + d, XS)], r1b.at[step, d - 1],
                s1s_sem.at[step, 2 + d], s1r_sem.at[step, 2 + d], on_x(d),
            ))
        return copies

    def stage2(step):
        copies = []
        for d in range(1, YS):
            copies.append(remote(
                s2a.at[step, mod(x + d, XS)], r2a.at[step, d - 1],
                s2s_sem.at[step, d - 1], s2r_sem.at[step, d - 1], on_x(d),
            ))
            copies.append(remote(
                s2b.at[step, mod(y + d, YS)], r2b.at[step, d - 1],
                s2s_sem.at[step, 2 + d], s2r_sem.at[step, 2 + d], on_y(d),
            ))
        return copies

    def stage3(step):
        return remote(s3.at[step], r3.at[step], s3s_sem.at[step], s3r_sem.at[step], on_z(offset(step)))

    def table_xy():
        copies = []
        for d in range(1, YS):
            copies.append(remote(tabz, taby.at[d - 1], txs_sem.at[d - 1], txr_sem.at[d - 1], on_y(d)))
            copies.append(remote(tabz, tabx.at[d - 1], txs_sem.at[2 + d], txr_sem.at[2 + d], on_x(d)))
        return copies

    def produce(step):
        x_local(step).wait()
        x_arrival(step).wait_recv()

        def multiply(j, carry):
            columns = pl.ds(pl.multiple_of(j * NODES, NODES), NODES)
            low = xbuf[step, 0, :, :, columns].reshape(HALF, NODES)
            high = xbuf[step, 1, :, :, columns].reshape(HALF, NODES)
            rows = jnp.concatenate([low, high], axis=0)
            product = jnp.dot(rows, pbuf[step, j], preferred_element_type=jnp.float32)
            fbuf[j] = product.astype(jnp.bfloat16)
            return carry

        lax.fori_loop(0, BLOCKS, multiply, 0)

        def pick(owner, carry):
            oy, ox = owner // XS, lax.rem(owner, XS)
            for rank in range(CAP):
                block = tabz[step, owner * CAP + rank]
                face = fbuf[block]
                s1a[step, oy, ox * CAP + rank] = face[:HALF]
                s1b[step, ox, oy * CAP + rank] = face[HALF:]
            return carry

        lax.fori_loop(0, OWNERS, pick, 0)
        for copy in stage1(step):
            copy.start()

    def merge_first(step, own, theirs, own_table, their_tables, merged, index, here, owner_of):
        def one(lane, carry):
            totals = [jnp.zeros((HALF, NODES), jnp.float32) for _ in range(SLOTS)]
            owner = owner_of(lane)
            for source in range(YS):
                for rank in range(CAP):
                    slot = OWNERS * CAP + owner * CAP + rank
                    if source == 0:
                        tag = own_table[step, slot]
                        value = own[step, here, lane * CAP + rank]
                    else:
                        tag = their_tables[source - 1, step, slot]
                        value = theirs[step, source - 1, lane * CAP + rank]
                    value = value.astype(jnp.float32)
                    for s in range(SLOTS):
                        totals[s] = totals[s] + value * (tag == s).astype(jnp.float32)
            for s in range(SLOTS):
                merged[step, lane, s] = totals[s].astype(jnp.bfloat16)
            return carry

        lax.fori_loop(0, XS, one, 0)

    def merge1(step):
        for copy in stage1(step):
            copy.wait_recv()
        merge_first(step, s1a, r1a, tabz, taby, s2a, 0, y, lambda lane: y * XS + lane)
        merge_first(step, s1b, r1b, tabz, tabx, s2b, 1, x, lambda lane: lane * XS + x)
        for copy in stage2(step):
            copy.start()

    def merge2(step):
        for copy in stage2(step):
            copy.wait_recv()
        for half, (own, theirs, here) in enumerate(((s2a, r2a, x), (s2b, r2b, y))):
            for s in range(SLOTS):
                total = own[step, here, s].astype(jnp.float32)
                for source in range(XS - 1):
                    total = total + theirs[step, source, s].astype(jnp.float32)
                s3[step, s, half] = total.astype(jnp.bfloat16)

        @pl.when(step > 0)
        def _():
            stage3(step).start()

    def advance(i, carry):
        @pl.when(i < STEPS)
        def _():
            @pl.when(i == 0)
            def _():
                p_local.wait()

            @pl.when((lax.rem(i, 2) == 1) & (i < STEPS - 1))
            def _():
                p_arrival(i).wait_recv()
                p_arrival(i + 1).wait_recv()

                @pl.when(i < STEPS - 3)
                def _():
                    forward(i, -1).start()
                    forward(i + 1, 1).start()

                @pl.when(i == STEPS - 3)
                def _():
                    last_low.start()
                    last_high.start()

            @pl.when(i == STEPS - 1)
            def _():
                last_low.wait_recv()
                last_high.wait_recv()

            @pl.when(i == 0)
            def _():
                t_local.wait()

            produce(i)

            @pl.when(i == 0)
            def _():
                def tables(step, carry):
                    table_z(step).wait_recv()
                    return carry

                lax.fori_loop(1, STEPS, tables, 0)
                for copy in table_xy():
                    copy.start()

        @pl.when((i >= 1) & (i < STEPS + 1))
        def _():
            @pl.when(i == 1)
            def _():
                for copy in table_xy():
                    copy.wait_recv()

            merge1(i - 1)

        @pl.when(i >= 2)
        def _():
            merge2(i - 2)

        return carry

    lax.fori_loop(0, STEPS + 2, advance, 0)

    def finish(step, carry):
        source_z = mod(z - offset(step), ZS)

        def place(ref):
            for s in range(SLOTS):
                for half in range(CS):
                    value = ref[step, s, half].astype(jnp.float32) * weight[pl.ds(s, 1), :]
                    value = value.astype(jnp.bfloat16).reshape(COMP, ROWS, NODES)
                    first = pl.multiple_of(source_z * (CS * ROWS) + half * ROWS, ROWS)
                    out[s, :, pl.ds(first, ROWS), :] = value

        @pl.when(step == 0)
        def _():
            place(s3)

        @pl.when(step > 0)
        def _():
            stage3(step).wait_recv()
            place(r3)

        return carry

    lax.fori_loop(0, STEPS, finish, 0)

    x_remote(0).wait_send()
    for copy in p_first:
        copy.wait_send()

    def drain(step, carry):
        table_z(step).wait_send()
        x_remote(step).wait_send()
        stage3(step).wait_send()
        return carry

    lax.fori_loop(1, STEPS, drain, 0)
    for step in (1, 3):
        forward(step, -1).wait_send()
        forward(step + 1, 1).wait_send()
    last_low.wait_send()
    last_high.wait_send()
    for copy in table_xy():
        copy.wait_send()

    def drain_xy(step, carry):
        for copy in stage1(step):
            copy.wait_send()
        for copy in stage2(step):
            copy.wait_send()
        return carry

    lax.fori_loop(0, STEPS, drain_xy, 0)


def fused(traces, projection, table, weight):
    bf16 = jnp.bfloat16
    dma = pltpu.SemaphoreType.DMA
    peers = (YS - 1) + (XS - 1)
    any_space = pl.BlockSpec(memory_space=pl.ANY)
    vmem = pl.BlockSpec(memory_space=pltpu.VMEM)
    return pl.pallas_call(
        kernel,
        out_shape=jax.ShapeDtypeStruct((SLOTS, COMP, ZS * CS * ROWS, NODES), bf16),
        in_specs=[any_space, any_space, pl.BlockSpec(memory_space=pltpu.SMEM), vmem],
        out_specs=vmem,
        scratch_shapes=[
            pltpu.VMEM((STEPS, CS, COMP, ROWS, COLS), bf16),
            pltpu.VMEM((STEPS, BLOCKS, NODES, NODES), bf16),
            pltpu.VMEM((BLOCKS, CS * HALF, NODES), bf16),
            pltpu.VMEM((STEPS, YS, XS * CAP, HALF, NODES), bf16),
            pltpu.VMEM((STEPS, XS, YS * CAP, HALF, NODES), bf16),
            pltpu.VMEM((STEPS, YS - 1, XS * CAP, HALF, NODES), bf16),
            pltpu.VMEM((STEPS, XS - 1, YS * CAP, HALF, NODES), bf16),
            pltpu.VMEM((STEPS, XS, SLOTS, HALF, NODES), bf16),
            pltpu.VMEM((STEPS, YS, SLOTS, HALF, NODES), bf16),
            pltpu.VMEM((STEPS, XS - 1, SLOTS, HALF, NODES), bf16),
            pltpu.VMEM((STEPS, YS - 1, SLOTS, HALF, NODES), bf16),
            pltpu.VMEM((STEPS, SLOTS, CS, HALF, NODES), bf16),
            pltpu.VMEM((STEPS, SLOTS, CS, HALF, NODES), bf16),
            pltpu.SMEM((STEPS, 2 * OWNERS * CAP), jnp.int32),
            pltpu.SMEM((YS - 1, STEPS, 2 * OWNERS * CAP), jnp.int32),
            pltpu.SMEM((XS - 1, STEPS, 2 * OWNERS * CAP), jnp.int32),
            dma((STEPS,)), dma((STEPS,)), dma((STEPS,)),
            dma((1,)), dma((STEPS + 1,)), dma((STEPS + 1,)),
            dma((1,)), dma((STEPS,)), dma((STEPS,)), dma((peers,)), dma((peers,)),
            dma((STEPS, peers)), dma((STEPS, peers)),
            dma((STEPS, peers)), dma((STEPS, peers)),
            dma((STEPS,)), dma((STEPS,)),
        ],
        compiler_params=pltpu.CompilerParams(
            collective_id=0, has_side_effects=True, vmem_limit_bytes=58 * 2**20
        ),
    )(traces, projection, table, weight)


def slot_table(owners, slots):
    same = owners[:, None] == owners[None, :]
    before = jnp.arange(BLOCKS)[None, :] < jnp.arange(BLOCKS)[:, None]
    rank = jnp.sum((same & before).astype(jnp.int32), axis=1)
    place = owners * CAP + rank
    chosen = place[None, :] == jnp.arange(OWNERS * CAP)[:, None]
    block = jnp.sum(jnp.where(chosen, jnp.arange(BLOCKS, dtype=jnp.int32)[None, :], 0), axis=1)
    tag = jnp.sum(jnp.where(chosen, slots[None, :] + 1, 0), axis=1) - 1
    return jnp.concatenate([block, tag]).astype(jnp.int32)


def per_device(traces, projection, owner_route, face_slot, face_weight):
    table = slot_table(owner_route[0, :, 0], face_slot[0, :, 0])
    return fused(traces, projection, table, face_weight)


def solution(mesh):
    return jax.shard_map(
        per_device,
        mesh=mesh,
        in_specs=(
            P(None, "tm", "box"),
            P("box", "tm", None, None),
            P("box", "tm", None),
            P("box", "tm", None),
            P(("tm", "box"), None),
        ),
        out_specs=P(("tm", "box"), None, None, None),
        check_vma=False,
    )
```

time: 232 us -> 92.8 us (0.40)
  the two profiles are of different devices: /device:TPU:1 before, /device:TPU:32 now
where the time goes in v1:
time: 92.8 us; the launch traced here: 92 us
  Pallas kernels  87 us (94%)
  other arithmetic  2.91 us (3%)
  local copies, waits for them, and re-layouts  2.09 us (2%)
    pallas_call x1, Pallas kernels, fused(): pl.pallas_call(kernel, out_shape=jax.ShapeDtypeStruct((SLOTS, COMP, ZS *...  87 us
    unnamed x1, local copies, waits for them, and re-layouts  2.09 us

profile of v1, /device:TPU:32, one launch (start us, length us, event | category | flops | bytes accessed | tf_op | source)
XLA Modules:
  0.0 92.0 jit_solution(4838419330228022231)
XLA Ops:
  0.0 0.7 add_bitcast_fusion
  0.7 0.9 convert_reduce_fusion
  1.6 0.7 multiply_add_fusion
  2.2 0.1 select_reduce_fusion.1
  2.3 0.6 pad_add_fusion.table
  2.9 87.0 %shard_map.55 = bf16[4,6,128,128]{3,2,1,0:T(8,128)(2,1)} custom-call(bf16[6,8,32768]{2,1,0:T(8,128)(2,1)} %traces.1, bf16[1,16,128,128]{3,2,1,0:T(8,128)(2,1)} %projection.1, s32[64]{0:T(128)} %pad_add_fusion.table, f32[4,128]{1,0:T(4,128)} %weight.1), custom_call_target="tpu_custom_call" | custom-call | tf_op jit(solution)/shard_map/pallas_call | solution.py:359
  89.9 2.1 %copy.7 = bf16[4,6,128,128]{3,2,1,0:T(8,128)(2,1)} copy(bf16[4,6,128,128]{3,2,1,0:T(8,128)(2,1)} %shard_map.55) | data formatting | bytes 1572864
  (1 shorter events, 0.0 us)

commit v2 on v1

v2 whole, which is shorter than its diff:
```python
import functools

import jax
import jax.numpy as jnp
from jax import lax
from jax.experimental import pallas as pl
from jax.experimental.pallas import tpu as pltpu
from jax.sharding import PartitionSpec as P

MESH = pl.DeviceIdType.MESH
ZS, CS, YS, XS = 8, 2, 4, 4
BLOCKS = 16
OWNERS = YS * XS
CAP = 2
SLOTS = 4
COMP = 6
ROWS = 8
NODES = 128
HALF = COMP * ROWS
COLS = BLOCKS * NODES
STEPS = ZS
FAR = 6
PLUS = (0, 1, 3, 5, FAR)
MINUS = (0, 2, 4, 7, FAR)


def mod(value, size):
    return lax.rem(value + size, jnp.int32(size))


def kernel(
    traces, projection, owners, slots, weight, out,
    xbuf, pbuf, fbuf, s1a, s1b, r1a, r1b, s2a, s2b, r2a, r2b, s3, r3,
    tabz, taby, tabx,
    xl_sem, xs_sem, xr_sem, pl_sem, ps_sem, pr_sem, tzs_sem, tzr_sem, txs_sem, txr_sem,
    s1s_sem, s1r_sem, s2s_sem, s2r_sem, s3s_sem, s3r_sem,
):
    tm = lax.axis_index("tm")
    box = lax.axis_index("box")
    z, c = tm // CS, lax.rem(tm, CS)
    y, x = box // XS, lax.rem(box, XS)
    sign = 1 - 2 * c

    def offset(step):
        place = step + (step // FAR) * (1 - 2 * (step // (FAR + 1)))
        return sign * ((place + 1) // 2) * (2 * lax.rem(place, 2) - 1)

    def at(zz, cc, yy, xx):
        return {"tm": zz * CS + cc, "box": yy * XS + xx}

    sibling = at(z, 1 - c, y, x)

    def on_z(dz):
        return at(mod(z + dz, ZS), c, y, x)

    def on_y(dy):
        return at(z, c, mod(y + dy, YS), x)

    def on_x(dx):
        return at(z, c, y, mod(x + dx, XS))

    def remote(src, dst, send, recv, device):
        return pltpu.make_async_remote_copy(
            src_ref=src, dst_ref=dst, send_sem=send, recv_sem=recv, device_id=device, device_id_type=MESH
        )

    def cols(way, core):
        return pl.ds(pl.multiple_of((mod(z + way, ZS) * CS + core) * COLS, COLS), COLS)

    def x_local(step):
        return pltpu.make_async_copy(traces.at[:, :, cols(offset(step), c)], xbuf.at[step, c], xl_sem.at[step])

    def x_remote(step):
        return remote(
            traces.at[:, :, cols(-offset(step), 1 - c)], xbuf.at[step, c], xs_sem.at[step], xr_sem.at[step], sibling
        )

    def x_arrival(step):
        return remote(
            traces.at[:, :, cols(-offset(step), 1 - c)], xbuf.at[step, 1 - c], xs_sem.at[step], xr_sem.at[step], sibling
        )

    p_local = pltpu.make_async_copy(projection.at[0], pbuf.at[0], pl_sem.at[0])

    def start_local(step, carry):
        x_local(step).start()
        return carry

    x_local(0).start()
    p_local.start()
    lax.fori_loop(1, STEPS, start_local, 0)
    barrier = pltpu.get_barrier_semaphore()
    pl.semaphore_signal(barrier, inc=1, device_id=sibling, device_id_type=MESH)
    for dz in (1, ZS - 1):
        pl.semaphore_signal(barrier, inc=1, device_id=on_z(dz), device_id_type=MESH)
    for d in range(1, YS):
        pl.semaphore_signal(barrier, inc=1, device_id=on_y(d), device_id_type=MESH)
        pl.semaphore_signal(barrier, inc=1, device_id=on_x(d), device_id_type=MESH)

    owner_of_block = [owners[j] for j in range(BLOCKS)]
    code_of_block = [slots[j] + SLOTS * j for j in range(BLOCKS)]

    def own_slots(owner, carry):
        none = jnp.int32(SLOTS * BLOCKS)
        first, last = none, jnp.int32(-1)
        for j in range(BLOCKS):
            match = owner_of_block[j] == owner
            first = jnp.where(match, jnp.minimum(first, code_of_block[j]), first)
            last = jnp.where(match, code_of_block[j], last)
        some, two = first < none, last > first
        first, last = jnp.where(some, first, 0), jnp.where(two, last, 0)
        tabz[0, owner * CAP] = first // SLOTS
        tabz[0, owner * CAP + 1] = last // SLOTS
        tabz[0, OWNERS * CAP + owner * CAP] = jnp.where(some, lax.rem(first, SLOTS), -1)
        tabz[0, OWNERS * CAP + owner * CAP + 1] = jnp.where(two, lax.rem(last, SLOTS), -1)
        return carry

    lax.fori_loop(0, OWNERS, own_slots, 0)
    pl.semaphore_wait(barrier, 1 + 2 + (YS - 1) + (XS - 1))

    half_p = BLOCKS // 2
    low, high = pl.ds(0, half_p), pl.ds(half_p, half_p)

    def ring(hop, turn):
        copies = []
        for way, steps, halves, there in ((0, PLUS, (low, high), -sign), (1, MINUS, (high, low), sign)):
            part = halves[turn]
            src = projection.at[0, part] if hop == 1 else pbuf.at[steps[hop - 1], part]
            copies.append(remote(
                src, pbuf.at[steps[hop], part], ps_sem.at[way, turn, hop - 1], pr_sem.at[way, turn, hop - 1], on_z(there)
            ))
        return copies

    def ring_table(hop):
        copies = []
        for steps, there in ((PLUS, -sign), (MINUS, sign)):
            if hop < 4 or steps is PLUS:
                step = steps[hop]
                copies.append(remote(
                    tabz.at[steps[hop - 1]], tabz.at[step], tzs_sem.at[step], tzr_sem.at[step], on_z(there)
                ))
        return copies

    x_remote(0).start()
    for copy in ring(1, 0) + ring_table(1) + ring(1, 1):
        copy.start()

    def start_remote(step, carry):
        x_remote(step).start()
        return carry

    lax.fori_loop(1, STEPS, start_remote, 0)

    def pass_on(hop, turn):
        arrived = ring(hop, turn) + (ring_table(hop) if turn == 0 else [])
        for copy in arrived:
            copy.wait_recv()
        if hop < 3 or (hop == 3 and turn == 0):
            for copy in ring(hop + 1, turn) + (ring_table(hop + 1) if turn == 0 else []):
                copy.start()

    def stage1(step):
        copies = []
        for d in range(1, YS):
            copies.append(remote(
                s1a.at[step, mod(y + d, YS)], r1a.at[step, d - 1],
                s1s_sem.at[step, d - 1], s1r_sem.at[step, d - 1], on_y(d),
            ))
            copies.append(remote(
                s1b.at[step, mod(x + d, XS)], r1b.at[step, d - 1],
                s1s_sem.at[step, 2 + d], s1r_sem.at[step, 2 + d], on_x(d),
            ))
        return copies

    def stage2(step):
        copies = []
        for d in range(1, YS):
            copies.append(remote(
                s2a.at[step, mod(x + d, XS)], r2a.at[step, d - 1],
                s2s_sem.at[step, d - 1], s2r_sem.at[step, d - 1], on_x(d),
            ))
            copies.append(remote(
                s2b.at[step, mod(y + d, YS)], r2b.at[step, d - 1],
                s2s_sem.at[step, 2 + d], s2r_sem.at[step, 2 + d], on_y(d),
            ))
        return copies

    def stage3(step):
        return remote(s3.at[step], r3.at[step], s3s_sem.at[step], s3r_sem.at[step], on_z(offset(step)))

    def table_xy(step):
        copies = []
        for d in range(1, YS):
            copies.append(remote(
                tabz.at[step], taby.at[step, d - 1], txs_sem.at[step, d - 1], txr_sem.at[step, d - 1], on_y(d)
            ))
            copies.append(remote(
                tabz.at[step], tabx.at[step, d - 1], txs_sem.at[step, 2 + d], txr_sem.at[step, 2 + d], on_x(d)
            ))
        return copies

    def produce(step):
        x_local(step).wait()
        x_arrival(step).wait_recv()

        def multiply(j, carry):
            columns = pl.ds(pl.multiple_of(j * NODES, NODES), NODES)
            low = xbuf[step, 0, :, :, columns].reshape(HALF, NODES)
            high = xbuf[step, 1, :, :, columns].reshape(HALF, NODES)
            rows = jnp.concatenate([low, high], axis=0)
            product = jnp.dot(rows, pbuf[step, j], preferred_element_type=jnp.float32)
            fbuf[j] = product.astype(jnp.bfloat16)
            return carry

        lax.fori_loop(0, BLOCKS, multiply, 0, unroll=4)

        def pick(owner, carry):
            oy, ox = owner // XS, lax.rem(owner, XS)
            for rank in range(CAP):
                block = tabz[step, owner * CAP + rank]
                face = fbuf[block]
                s1a[step, oy, ox * CAP + rank] = face[:HALF]
                s1b[step, ox, oy * CAP + rank] = face[HALF:]
            return carry

        lax.fori_loop(0, OWNERS, pick, 0)
        for copy in table_xy(step) + stage1(step):
            copy.start()

    def merge_first(step, own, theirs, own_table, their_tables, merged, index, here, owner_of):
        def one(lane, carry):
            totals = [jnp.zeros((HALF, NODES), jnp.float32) for _ in range(SLOTS)]
            owner = owner_of(lane)
            for source in range(YS):
                for rank in range(CAP):
                    slot = OWNERS * CAP + owner * CAP + rank
                    if source == 0:
                        tag = own_table[step, slot]
                        value = own[step, here, lane * CAP + rank]
                    else:
                        tag = their_tables[step, source - 1, slot]
                        value = theirs[step, source - 1, lane * CAP + rank]
                    value = value.astype(jnp.float32)
                    for s in range(SLOTS):
                        totals[s] = totals[s] + value * (tag == s).astype(jnp.float32)
            for s in range(SLOTS):
                merged[step, lane, s] = totals[s].astype(jnp.bfloat16)
            return carry

        lax.fori_loop(0, XS, one, 0)

    def merge1(step):
        for copy in table_xy(step) + stage1(step):
            copy.wait_recv()
        merge_first(step, s1a, r1a, tabz, taby, s2a, 0, y, lambda lane: y * XS + lane)
        merge_first(step, s1b, r1b, tabz, tabx, s2b, 1, x, lambda lane: lane * XS + x)
        for copy in stage2(step):
            copy.start()

    def merge2(step):
        for copy in stage2(step):
            copy.wait_recv()
        for half, (own, theirs, here) in enumerate(((s2a, r2a, x), (s2b, r2b, y))):
            for s in range(SLOTS):
                total = own[step, here, s].astype(jnp.float32)
                for source in range(XS - 1):
                    total = total + theirs[step, source, s].astype(jnp.float32)
                s3[step, s, half] = total.astype(jnp.bfloat16)

        @pl.when(step == 2)
        def _():
            stage3(1).start()

        @pl.when(step > 1)
        def _():
            stage3(step).start()

    def advance(i, carry):
        @pl.when(i < STEPS)
        def _():
            @pl.when(i == 0)
            def _():
                p_local.wait()

            @pl.when(i == 1)
            def _():
                merge1(0)

            for hop in range(1, 4):
                @pl.when(i == 2 * hop - 1)
                def _(hop=hop):
                    pass_on(hop, 1)

            @pl.when(i == FAR)
            def _():
                pass_on(4, 0)

            produce(i)

            for hop in range(1, 4):
                @pl.when(i == 2 * hop - 2)
                def _(hop=hop):
                    pass_on(hop, 0)

        @pl.when((i >= 2) & (i < STEPS + 1))
        def _():
            merge1(i - 1)

        @pl.when(i >= 2)
        def _():
            merge2(i - 2)

        return carry

    lax.fori_loop(0, STEPS + 2, advance, 0)

    def finish(step, carry):
        source_z = mod(z - offset(step), ZS)

        def place(ref):
            for s in range(SLOTS):
                for half in range(CS):
                    value = ref[step, s, half].astype(jnp.float32) * weight[pl.ds(s, 1), :]
                    value = value.astype(jnp.bfloat16).reshape(COMP, ROWS, NODES)
                    first = pl.multiple_of(source_z * (CS * ROWS) + half * ROWS, ROWS)
                    out[s, :, pl.ds(first, ROWS), :] = value

        @pl.when(step == 0)
        def _():
            place(s3)

        @pl.when(step > 0)
        def _():
            stage3(step).wait_recv()
            place(r3)

        return carry

    lax.fori_loop(0, STEPS, finish, 0)

    for hop in range(1, 5):
        for copy in ring(hop, 0) + ring_table(hop) + (ring(hop, 1) if hop < 4 else []):
            copy.wait_send()

    def drain(step, carry):
        @pl.when(step > 0)
        def _():
            stage3(step).wait_send()

        x_remote(step).wait_send()
        return carry

    lax.fori_loop(0, STEPS, drain, 0)

    def drain_xy(step, carry):
        for copy in table_xy(step) + stage1(step):
            copy.wait_send()
        for copy in stage2(step):
            copy.wait_send()
        return carry

    lax.fori_loop(0, STEPS, drain_xy, 0)


def fused(traces, projection, owners, slots, weight):
    bf16 = jnp.bfloat16
    dma = pltpu.SemaphoreType.DMA
    peers = (YS - 1) + (XS - 1)
    any_space = pl.BlockSpec(memory_space=pl.ANY)
    vmem = pl.BlockSpec(memory_space=pltpu.VMEM)
    smem = pl.BlockSpec(memory_space=pltpu.SMEM)
    return pl.pallas_call(
        kernel,
        out_shape=jax.ShapeDtypeStruct((SLOTS, COMP, ZS * CS * ROWS, NODES), bf16),
        in_specs=[any_space, any_space, smem, smem, vmem],
        out_specs=vmem,
        scratch_shapes=[
            pltpu.VMEM((STEPS, CS, COMP, ROWS, COLS), bf16),
            pltpu.VMEM((STEPS, BLOCKS, NODES, NODES), bf16),
            pltpu.VMEM((BLOCKS, CS * HALF, NODES), bf16),
            pltpu.VMEM((STEPS, YS, XS * CAP, HALF, NODES), bf16),
            pltpu.VMEM((STEPS, XS, YS * CAP, HALF, NODES), bf16),
            pltpu.VMEM((STEPS, YS - 1, XS * CAP, HALF, NODES), bf16),
            pltpu.VMEM((STEPS, XS - 1, YS * CAP, HALF, NODES), bf16),
            pltpu.VMEM((STEPS, XS, SLOTS, HALF, NODES), bf16),
            pltpu.VMEM((STEPS, YS, SLOTS, HALF, NODES), bf16),
            pltpu.VMEM((STEPS, XS - 1, SLOTS, HALF, NODES), bf16),
            pltpu.VMEM((STEPS, YS - 1, SLOTS, HALF, NODES), bf16),
            pltpu.VMEM((STEPS, SLOTS, CS, HALF, NODES), bf16),
            pltpu.VMEM((STEPS, SLOTS, CS, HALF, NODES), bf16),
            pltpu.SMEM((STEPS, 2 * OWNERS * CAP), jnp.int32),
            pltpu.SMEM((STEPS, YS - 1, 2 * OWNERS * CAP), jnp.int32),
            pltpu.SMEM((STEPS, XS - 1, 2 * OWNERS * CAP), jnp.int32),
            dma((STEPS,)), dma((STEPS,)), dma((STEPS,)),
            dma((1,)), dma((2, 2, 4)), dma((2, 2, 4)),
            dma((STEPS,)), dma((STEPS,)), dma((STEPS, peers)), dma((STEPS, peers)),
            dma((STEPS, peers)), dma((STEPS, peers)),
            dma((STEPS, peers)), dma((STEPS, peers)),
            dma((STEPS,)), dma((STEPS,)),
        ],
        compiler_params=pltpu.CompilerParams(
            collective_id=0, has_side_effects=True, vmem_limit_bytes=58 * 2**20
        ),
    )(traces, projection, owners, slots, weight)


def per_device(traces, projection, owner_route, face_slot, face_weight):
    return fused(traces, projection, owner_route[0, :, 0], face_slot[0, :, 0], face_weight)


def solution(mesh):
    return jax.shard_map(
        per_device,
        mesh=mesh,
        in_specs=(
            P(None, "tm", "box"),
            P("box", "tm", None, None),
            P("box", "tm", None),
            P("box", "tm", None),
            P(("tm", "box"), None),
        ),
        out_specs=P(("tm", "box"), None, None, None),
        check_vma=False,
    )
```

time: 92.8 us -> 86.8 us (0.935)
  other arithmetic: 2.91 us -> 0 us
  Pallas kernels: 87 us -> 84.6 us
    pallas_call x1, Pallas kernels: 87 us -> 84.6 us  [fused(): pl.pallas_call(kernel, out_shape=jax.ShapeDtypeStruct((SLOTS, COMP, ZS *...]
    add x2 -> x0, other arithmetic: 1.32 us -> none  [the longest x1 0.66 us: slot_table(): place = owners * CAP + rank]
    reduce_sum x2 -> x0, other arithmetic: 1 us -> none  [the longest x1 0.91 us: slot_table(): rank = jnp.sum((same & before).astype(jnp.int32), axis=1)]
where the time goes in v2:
time: 86.8 us; the launch traced here: 86.7 us
  Pallas kernels  84.6 us (97%)
  local copies, waits for them, and re-layouts  2.09 us (2%)
    pallas_call x1, Pallas kernels, fused(): pl.pallas_call(kernel, out_shape=jax.ShapeDtypeStruct((SLOTS, COMP, ZS *...  84.6 us
    unnamed x1, local copies, waits for them, and re-layouts  2.09 us

profile of v2, /device:TPU:32, one launch (start us, length us, event | category | flops | bytes accessed | tf_op | source)
XLA Modules:
  0.0 86.7 jit_solution(16538727637488463660)
XLA Ops:
  0.0 84.6 %shard_map.55 = bf16[4,6,128,128]{3,2,1,0:T(8,128)(2,1)} custom-call(bf16[6,8,32768]{2,1,0:T(8,128)(2,1)} %traces.1, bf16[1,16,128,128]{3,2,1,0:T(8,128)(2,1)} %projection.1, s32[16]{0:T(128)} %bitcast.2, s32[16]{0:T(128)} %bitcast.3, f32[4,128]{1,0:T(4,128)} %weight.1), custom_call_target="tpu_custom_call" | custom-call | tf_op jit(solution)/shard_map/pallas_call | solution.py:372
  84.6 2.1 %copy.7 = bf16[4,6,128,128]{3,2,1,0:T(8,128)(2,1)} copy(bf16[4,6,128,128]{3,2,1,0:T(8,128)(2,1)} %shard_map.55) | data formatting | bytes 1572864

commit v3 on v2

--- a/solution.py
+++ b/solution.py
@@ -1,5 +1,3 @@
-import functools
-
 import jax
 import jax.numpy as jnp
 from jax import lax
@@ -212,7 +210,7 @@
             fbuf[j] = product.astype(jnp.bfloat16)
             return carry
 
-        lax.fori_loop(0, BLOCKS, multiply, 0, unroll=4)
+        lax.fori_loop(0, BLOCKS, multiply, 0, unroll=16)
 
         def pick(owner, carry):
             oy, ox = owner // XS, lax.rem(owner, XS)
@@ -371,7 +369,7 @@
     smem = pl.BlockSpec(memory_space=pltpu.SMEM)
     return pl.pallas_call(
         kernel,
-        out_shape=jax.ShapeDtypeStruct((SLOTS, COMP, ZS * CS * ROWS, NODES), bf16),
+        out_shape=pltpu.VMEM((SLOTS, COMP, ZS * CS * ROWS, NODES), bf16),
         in_specs=[any_space, any_space, smem, smem, vmem],
         out_specs=vmem,
         scratch_shapes=[

time: 86.8 us -> 84.3 us (0.971)
  Pallas kernels: 84.6 us -> 83.3 us
  local copies, waits for them, and re-layouts: 2.09 us -> 0.88 us
    pallas_call x1, Pallas kernels: 84.6 us -> 83.3 us  [fused(): pl.pallas_call(kernel, out_shape=pltpu.VMEM((SLOTS, COMP, ZS * CS * ROWS,...]
    unnamed x1, local copies, waits for them, and re-layouts: 2.09 us -> 0.88 us
where the time goes in v3:
time: 84.3 us; the launch traced here: 84.2 us
  Pallas kernels  83.3 us (99%)
  local copies, waits for them, and re-layouts  0.88 us (1%)
    pallas_call x1, Pallas kernels, fused(): pl.pallas_call(kernel, out_shape=pltpu.VMEM((SLOTS, COMP, ZS * CS * ROWS,...  83.3 us

profile of v3, /device:TPU:32, one launch (start us, length us, event | category | flops | bytes accessed | tf_op | source)
XLA Modules:
  0.0 84.2 jit_solution(16374897589541788443)
XLA Ops:
  0.0 83.3 %shard_map.55 = bf16[4,6,128,128]{3,2,1,0:T(8,128)(2,1)S(1)} custom-call(bf16[6,8,32768]{2,1,0:T(8,128)(2,1)} %traces.1, bf16[1,16,128,128]{3,2,1,0:T(8,128)(2,1)} %projection.1, s32[16]{0:T(128)} %bitcast.2, s32[16]{0:T(128)} %bitcast.3, f32[4,128]{1,0:T(4,128)} %weight.1), custom_call_target="tpu_custom_call" | custom-call | tf_op jit(solution)/shard_map/pallas_call | solution.py:370
  83.3 0.9 %copy.7 = bf16[4,6,128,128]{3,2,1,0:T(8,128)(2,1)} copy(bf16[4,6,128,128]{3,2,1,0:T(8,128)(2,1)S(1)} %shard_map.55) | data formatting | bytes 1572864

commit v4 on v3

--- a/solution.py
+++ b/solution.py
@@ -221,9 +221,36 @@
                 s1b[step, ox, oy * CAP + rank] = face[HALF:]
             return carry
 
-        lax.fori_loop(0, OWNERS, pick, 0)
+        lax.fori_loop(0, OWNERS, pick, 0, unroll=4)
         for copy in table_xy(step) + stage1(step):
             copy.start()
+
+    def produce_own(core):
+        def multiply(j, carry):
+            columns = pl.ds(pl.multiple_of(j * NODES, NODES), NODES)
+            rows = xbuf[0, core, :, :, columns].reshape(HALF, NODES)
+            product = jnp.dot(rows, pbuf[0, j], preferred_element_type=jnp.float32)
+            fbuf[j, pl.ds(pl.multiple_of(core * HALF, HALF), HALF)] = product.astype(jnp.bfloat16)
+            return carry
+
+        lax.fori_loop(0, BLOCKS, multiply, 0, unroll=16)
+
+        for half in range(CS):
+            @pl.when(core == half)
+            def _(half=half):
+                def pick(owner, carry):
+                    oy, ox = owner // XS, lax.rem(owner, XS)
+                    for rank in range(CAP):
+                        face = fbuf[tabz[0, owner * CAP + rank], half * HALF : (half + 1) * HALF]
+                        if half == 0:
+                            s1a[0, oy, ox * CAP + rank] = face
+                        else:
+                            s1b[0, ox, oy * CAP + rank] = face
+                    return carry
+
+                lax.fori_loop(0, OWNERS, pick, 0)
+                for copy in stage1(0)[half::CS]:
+                    copy.start()
 
     def merge_first(step, own, theirs, own_table, their_tables, merged, index, here, owner_of):
         def one(lane, carry):
@@ -245,7 +272,7 @@
                 merged[step, lane, s] = totals[s].astype(jnp.bfloat16)
             return carry
 
-        lax.fori_loop(0, XS, one, 0)
+        lax.fori_loop(0, XS, one, 0, unroll=2)
 
     def merge1(step):
         for copy in table_xy(step) + stage1(step):
@@ -265,11 +292,7 @@
                     total = total + theirs[step, source, s].astype(jnp.float32)
                 s3[step, s, half] = total.astype(jnp.bfloat16)
 
-        @pl.when(step == 2)
-        def _():
-            stage3(1).start()
-
-        @pl.when(step > 1)
+        @pl.when(step > 0)
         def _():
             stage3(step).start()
 
@@ -293,7 +316,18 @@
             def _():
                 pass_on(4, 0)
 
-            produce(i)
+            @pl.when(i == 0)
+            def _():
+                x_local(0).wait()
+                produce_own(c)
+                for copy in table_xy(0):
+                    copy.start()
+                x_arrival(0).wait_recv()
+                produce_own(1 - c)
+
+            @pl.when(i > 0)
+            def _():
+                produce(i)
 
             for hop in range(1, 4):
                 @pl.when(i == 2 * hop - 2)

time: 84.3 us -> 83.7 us (level)
  no operation moved by 1% of the time
where the time goes in v4:
time: 83.7 us; the launch traced here: 83.6 us
  Pallas kernels  82.7 us (99%)
  local copies, waits for them, and re-layouts  0.88 us (1%)
    pallas_call x1, Pallas kernels, fused(): pl.pallas_call(kernel, out_shape=pltpu.VMEM((SLOTS, COMP, ZS * CS * ROWS,...  82.7 us

profile of v4, /device:TPU:32, one launch (start us, length us, event | category | flops | bytes accessed | tf_op | source)
XLA Modules:
  0.0 83.6 jit_solution(7736454231888873136)
XLA Ops:
  0.0 82.7 %shard_map.55 = bf16[4,6,128,128]{3,2,1,0:T(8,128)(2,1)S(1)} custom-call(bf16[6,8,32768]{2,1,0:T(8,128)(2,1)} %traces.1, bf16[1,16,128,128]{3,2,1,0:T(8,128)(2,1)} %projection.1, s32[16]{0:T(128)} %bitcast.2, s32[16]{0:T(128)} %bitcast.3, f32[4,128]{1,0:T(4,128)} %weight.1), custom_call_target="tpu_custom_call" | custom-call | tf_op jit(solution)/shard_map/pallas_call | solution.py:404
  82.7 0.9 %copy.7 = bf16[4,6,128,128]{3,2,1,0:T(8,128)(2,1)} copy(bf16[4,6,128,128]{3,2,1,0:T(8,128)(2,1)S(1)} %shard_map.55) | data formatting | bytes 1572864
